TPU v7x, 256 devices: a whole 4x4x8 slice. The times are simulated.
256 devices in a mesh: row: 8 (over x, core), col: 32 (over y, z).
Axes of the slice: x: 4, y: 4, z: 8, core: 2. Of those that a mesh axis runs over, the one named last changes fastest.
Arguments:
- grid_points: int32 [2, 6, 4096], P(None, None, 'row'), may hold values from 0 to 127
- variable: int32 [6, 4096], P(None, 'row'), may hold values from 0 to 2
Outputs:
- panel_factor: float32 [6, 4096, 1536], P(None, ('row', 'col'))
- trailing: float32 [6, 4096, 16384], P(None, 'row', 'col')
All inputs are finite; a program needn't handle non-finite values.
Results may differ from a plain program's by a relative error of at most 0.0042.
Values may be sent and summed in bfloat16 or wider, within the bound.
A program may use at most 128 MiB of HBM per device.

v0:
```python
import jax
import jax.numpy as jnp
from jax import lax
from jax.sharding import PartitionSpec as P

PANELS = 3
GRID = 128


range_scale = 0.05
nugget = 0.5
rho_first = 0.35
rho_second = 0.2
rho_third = 0.3
highest = lax.Precision.HIGHEST


def rows_first(arrays, axis, dims):
    turned = [jnp.moveaxis(a, dim, 0) for a, dim in zip(arrays, dims)]
    widths = [t[0].size for t in turned]
    both = jnp.concatenate([t.reshape(-1, w) for t, w in zip(turned, widths)], axis=1)
    whole = lax.all_gather(both, axis, axis=0, tiled=True)
    parts = jnp.split(whole, [sum(widths[:k]) for k in range(1, len(widths))], axis=1)
    return tuple(
        (
            jnp.moveaxis(b.reshape(-1, *t.shape[1:]), 0, dim)
            for b, t, dim in zip(parts, turned, dims)
        )
    )


def kind_scale(kinds):
    return jnp.where(kinds == 0, 1.0, jnp.where(kinds == 1, 1.3, 0.8))


def covariance(row_x, row_y, row_kind, col_x, col_y, col_kind):
    delta_x = (row_x[:, None] - col_x[None, :]).astype(jnp.float32)
    delta_y = (row_y[:, None] - col_y[None, :]).astype(jnp.float32)
    distance = jnp.sqrt(delta_x * delta_x + delta_y * delta_y) * (1.0 / (GRID * range_scale))
    order_sum = row_kind[:, None] + col_kind[None, :]
    dist_square = distance * distance
    dist_cube = dist_square * distance
    dist_fourth = dist_square * dist_square
    polynomial = jnp.where(order_sum == 0, 1.0, 1.0 + distance)
    polynomial = jnp.where(order_sum == 2, 1.0 + distance + dist_square / 3.0, polynomial)
    polynomial = jnp.where(
        order_sum == 3, 1.0 + distance + 0.4 * dist_square + dist_cube / 15.0, polynomial
    )
    polynomial = jnp.where(
        order_sum == 4,
        1.0 + distance + dist_square * (3.0 / 7.0) + dist_cube * (2.0 / 21.0) + dist_fourth / 105.0,
        polynomial,
    )
    correlation = jnp.where(
        row_kind[:, None] == col_kind[None, :],
        1.0,
        jnp.where(order_sum == 1, rho_first, jnp.where(order_sum == 2, rho_second, rho_third)),
    )
    scale_row = kind_scale(row_kind)
    scale_col = kind_scale(col_kind)
    return correlation * scale_row[:, None] * scale_col[None, :] * polynomial * jnp.exp(-distance)


def leading_factor(matrix, count, size):
    remaining = matrix
    lower_blocks = {}
    inverse_blocks = {}
    identity = jnp.eye(size, dtype=jnp.float32)
    for panel_step in range(count):
        row_begin = panel_step * size
        row_end = row_begin + size
        diag_factor = jnp.linalg.cholesky(remaining[row_begin:row_end, row_begin:row_end])
        diag_inverse = lax.linalg.triangular_solve(
            diag_factor, identity, left_side=True, lower=True
        )
        lower_blocks[panel_step, panel_step] = diag_factor
        inverse_blocks[panel_step, panel_step] = diag_inverse
        if panel_step + 1 < count:
            below_rows = jnp.dot(
                remaining[row_end:, row_begin:row_end], diag_inverse.T, precision=highest
            )
            for row_block in range(panel_step + 1, count):
                lower_blocks[row_block, panel_step] = below_rows[
                    (row_block - panel_step - 1) * size : (row_block - panel_step) * size
                ]
            trailing_part = remaining[row_end:, row_end:] - jnp.dot(
                below_rows, below_rows.T, precision=highest
            )
            remaining = remaining.at[row_end:, row_end:].set(trailing_part)
    for row_block in range(count):
        for col_block in range(row_block):
            running = jnp.zeros((size, size), jnp.float32)
            for mid_block in range(col_block, row_block):
                running = running + jnp.dot(
                    lower_blocks[row_block, mid_block],
                    inverse_blocks[mid_block, col_block],
                    precision=highest,
                )
            inverse_blocks[row_block, col_block] = -jnp.dot(
                inverse_blocks[row_block, row_block], running, precision=highest
            )
    zeros_block = jnp.zeros((size, size), jnp.float32)
    lower_rows = []
    inverse_rows = []
    for row_block in range(count):
        lower_rows.append(
            jnp.concatenate(
                [
                    lower_blocks[row_block, col_block] if col_block <= row_block else zeros_block
                    for col_block in range(count)
                ],
                1,
            )
        )
        inverse_rows.append(
            jnp.concatenate(
                [
                    inverse_blocks[row_block, col_block] if col_block <= row_block else zeros_block
                    for col_block in range(count)
                ],
                1,
            )
        )
    return (jnp.concatenate(lower_rows, 0), jnp.concatenate(inverse_rows, 0))


def local(grid_points, variable):
    rows_dev = variable.shape[0]
    tile_size = variable.shape[1]
    row_count = lax.axis_size("row")
    col_count = lax.axis_size("col")
    piece_rows = tile_size // col_count
    row_index = lax.axis_index("row")
    col_index = lax.axis_index("col")
    lead_size = PANELS * tile_size
    all_grid, all_kind = rows_first((grid_points, variable), "row", (2, 1))
    coord_x = all_grid[0].reshape(-1)
    coord_y = all_grid[1].reshape(-1)
    kinds = all_kind.reshape(-1)
    lead_x = coord_x[:lead_size]
    lead_y = coord_y[:lead_size]
    lead_kind = kinds[:lead_size]
    lead_cov = covariance(lead_x, lead_y, lead_kind, lead_x, lead_y, lead_kind)
    lead_cov = lead_cov + nugget * jnp.eye(lead_size, dtype=jnp.float32)
    lower_factor, inverse = leading_factor(lead_cov, PANELS, tile_size)
    offset = col_index * piece_rows
    mine_grid = lax.dynamic_slice_in_dim(grid_points, offset, piece_rows, 2)
    mine_kind = lax.dynamic_slice_in_dim(variable, offset, piece_rows, 1)
    piece_cov = covariance(
        mine_grid[0].reshape(-1),
        mine_grid[1].reshape(-1),
        mine_kind.reshape(-1),
        lead_x,
        lead_y,
        lead_kind,
    )
    solved = jnp.dot(piece_cov, inverse.T, precision=highest).reshape(
        rows_dev, piece_rows, lead_size
    )
    lead_rows = lax.dynamic_slice_in_dim(
        lower_factor,
        jnp.minimum(row_index * tile_size + offset, lead_size - piece_rows),
        piece_rows,
        0,
    )
    first_slot = jnp.where(row_index < PANELS, lead_rows, solved[0])
    panel_full = jnp.concatenate([first_slot[None], solved[1:]], 0)
    panel_half = panel_full.astype(jnp.bfloat16)
    target = PANELS + col_index
    col_start = target * tile_size
    col_x = lax.dynamic_slice_in_dim(coord_x, col_start, tile_size)
    col_y = lax.dynamic_slice_in_dim(coord_y, col_start, tile_size)
    col_kind = lax.dynamic_slice_in_dim(kinds, col_start, tile_size)
    row_iota = lax.broadcasted_iota(jnp.int32, (tile_size, tile_size), 0)
    col_iota = lax.broadcasted_iota(jnp.int32, (tile_size, tile_size), 1)

    def assemble(slot):
        cov_block = covariance(
            grid_points[0][slot], grid_points[1][slot], variable[slot], col_x, col_y, col_kind
        )
        equal = (slot * row_count + row_index == target) & (row_iota == col_iota)
        return jnp.where(equal, cov_block + nugget, cov_block)

    cov_tiles = lax.map(assemble, jnp.arange(rows_dev, dtype=jnp.int32))
    target_cov = covariance(col_x, col_y, col_kind, lead_x, lead_y, lead_kind)
    column_rows = jnp.dot(target_cov, inverse.T, precision=highest).astype(jnp.bfloat16)
    update = jnp.einsum(
        "sik,jk->sij",
        lax.all_gather(panel_half, "col", axis=1, tiled=True),
        column_rows,
        preferred_element_type=jnp.float32,
    )
    return (panel_full, cov_tiles - update)


def solution(mesh):
    return jax.shard_map(
        local,
        mesh=mesh,
        in_specs=(P(None, None, "row"), P(None, "row")),
        out_specs=(P(None, ("row", "col"), None), P(None, "row", "col")),
        check_vma=False,
    )
```

profile of v0, /device:TPU:1, one launch (start us, length us, event | category | flops | bytes accessed | tf_op | source)
XLA Modules:
  0.0 741.4 jit_solution(12981079836239768969)
XLA Ops:
  8.7 16.0 %all_gather.6 = s32[4096,18]{0,1:T(8,128)S(1)} all-gather(s32[512,18]{0,1:T(8,128)S(1)} %pad_add_fusion), channel_id=1, replica_groups=mesh['row'=8,'col'=32] {'row'}, dimensions={0}, use_global_device_ids=true | all-gather | bytes 331776 | tf_op jit(solution)/shard_map/all_gather | solution.py:22
  25.8 18.3 %fusion.28 = f32[1536,1536]{0,1:T(8,128)S(1)} fusion(s32[1536]{0:T(1024)S(1)} %slice.297, s32[1536]{0:T(1024)S(1)} %slice.295, f32[1536]{0:T(1024)S(1)} %select_select_fusion.5, s32[1536]{0:T(1024)S(1)} %slice.293), kind=kLoop, calls=%fused_computation.64 | loop fusion | flops 108527616 | bytes 9461760 | tf_op jit(solution)/shard_map/add | solution.py:144
  49.7 11.7 %cholesky.374 = f32[128,128]{1,0:T(8,128)S(1)} custom-call(f32[128,128]{1,0:T(8,128)S(1)} %cholesky.586), custom_call_target="Cholesky" | custom-call | tf_op jit(solution)/shard_map/jit(cholesky)/cholesky | solution.py:72
  72.1 11.7 %cholesky.393 = f32[128,128]{1,0:T(8,128)S(1)} custom-call(f32[128,128]{1,0:T(8,128)S(1)} %cholesky.590), custom_call_target="Cholesky" | custom-call | tf_op jit(solution)/shard_map/jit(cholesky)/cholesky | solution.py:72
  94.7 11.7 %cholesky.414 = f32[128,128]{1,0:T(8,128)S(1)} custom-call(f32[128,128]{1,0:T(8,128)S(1)} %cholesky.595), custom_call_target="Cholesky" | custom-call | tf_op jit(solution)/shard_map/jit(cholesky)/cholesky | solution.py:72
  117.5 11.7 %cholesky.431 = f32[128,128]{1,0:T(8,128)S(1)} custom-call(f32[128,128]{1,0:T(8,128)S(1)} %convolution_subtract_fusion.19), custom_call_target="Cholesky" | custom-call | tf_op jit(solution)/shard_map/jit(cholesky)/cholesky | solution.py:72
  142.5 39.3 %custom-call.34 = f32[4,128,128]{1,2,0:T(8,128)S(1)} custom-call(f32[4,128,128]{2,1,0:T(8,128)S(1)} %get-tuple-element.206), custom_call_target="InvertDiagBlocksLowerTriangular" | custom-call | tf_op jit(solution)/shard_map/triangular_solve/custom-call.3 | solution.py:73
  210.8 11.7 %cholesky.446 = f32[128,128]{1,0:T(8,128)S(1)} custom-call(f32[128,128]{1,0:T(8,128)S(1)} %cholesky.599), custom_call_target="Cholesky" | custom-call | tf_op jit(solution)/shard_map/jit(cholesky)/cholesky | solution.py:72
  245.7 11.9 %cholesky.465 = f32[128,128]{1,0:T(8,128)S(1)} custom-call(f32[128,128]{1,0:T(8,128)S(1)} %cholesky.603), custom_call_target="Cholesky" | custom-call | tf_op jit(solution)/shard_map/jit(cholesky)/cholesky | solution.py:72
  274.2 11.7 %cholesky.486 = f32[128,128]{1,0:T(8,128)S(1)} custom-call(f32[128,128]{1,0:T(8,128)S(1)} %cholesky.608), custom_call_target="Cholesky" | custom-call | tf_op jit(solution)/shard_map/jit(cholesky)/cholesky | solution.py:72
  299.4 12.1 %cholesky.503 = f32[128,128]{1,0:T(8,128)S(1)} custom-call(f32[128,128]{1,0:T(8,128)S(1)} %convolution_subtract_fusion.18), custom_call_target="Cholesky" | custom-call | tf_op jit(solution)/shard_map/jit(cholesky)/cholesky | solution.py:72
  329.1 39.9 %custom-call.38 = f32[4,128,128]{1,2,0:T(8,128)} custom-call(f32[4,128,128]{2,1,0:T(8,128)S(1)} %get-tuple-element.207), custom_call_target="InvertDiagBlocksLowerTriangular" | custom-call | tf_op jit(solution)/shard_map/triangular_solve/custom-call.3 | solution.py:73
  391.2 11.7 %cholesky.518 = f32[128,128]{1,0:T(8,128)S(1)} custom-call(f32[128,128]{1,0:T(8,128)S(1)} %cholesky.612), custom_call_target="Cholesky" | custom-call | tf_op jit(solution)/shard_map/jit(cholesky)/cholesky | solution.py:72
  433.9 11.7 %cholesky.537 = f32[128,128]{1,0:T(8,128)S(1)} custom-call(f32[128,128]{1,0:T(8,128)S(1)} %slice-done), custom_call_target="Cholesky" | custom-call | tf_op jit(solution)/shard_map/jit(cholesky)/cholesky | solution.py:72
  461.0 13.2 %cholesky.558 = f32[128,128]{1,0:T(8,128)} custom-call(f32[128,128]{1,0:T(8,128)} %cholesky.621), custom_call_target="Cholesky" | custom-call | tf_op jit(solution)/shard_map/jit(cholesky)/cholesky | solution.py:72
  489.9 11.7 %cholesky.575 = f32[128,128]{1,0:T(8,128)S(1)} custom-call(f32[128,128]{1,0:T(8,128)S(1)} %convolution_subtract_fusion.17), custom_call_target="Cholesky" | custom-call | tf_op jit(solution)/shard_map/jit(cholesky)/cholesky | solution.py:72
  506.3 12.0 %while.24 = (s32[]{:T(128)}, f32[512,512]{1,0:T(8,128)}, s32[4,2]{0,1:T(2,128)S(1)}, f32[4,128,128]{2,1,0:T(8,128)S(1)}, s32[]{:T(128)}) while((s32[]{:T(128)}, f32[512,512]{1,0:T(8,128)}, s32[4,2]{0,1:T(2,128)S(1)}, f32[4,128,128]{2,1,0:T(8,128)S(1)}, s32[]{:T(128)}) %tuple.138), condition=%wide.while_cond.2.clone.1, body=%wide.while_body.2.clone.1.sunk | while | flops 2 | bytes 131181 | solution.py:73
  518.3 39.7 %custom-call.42 = f32[4,128,128]{1,2,0:T(8,128)S(1)} custom-call(f32[4,128,128]{2,1,0:T(8,128)S(1)} %get-tuple-element.208), custom_call_target="InvertDiagBlocksLowerTriangular" | custom-call | tf_op jit(solution)/shard_map/triangular_solve/custom-call.3 | solution.py:73
  581.3 20.2 %fusion.38 = f32[1536,1536]{1,0:T(8,128)} fusion(f32[512,512]{1,0:T(8,128)S(1)} %cholesky.441, f32[512,512]{1,0:T(8,128)} %pad_maximum_fusion.1, f32[128,512]{1,0:T(8,128)S(1)} %fusion.240, f32[128,512]{1,0:T(8,128)} %copy-done.12, f32[128,512]{1,0:T(8,128)S(1)} %fusion.243, f32[128,512]{1,0:T(8,128)S(1)} %fusion.205, f32[512,512]{1,0:T(8,128)} %convolution_negate_fusion, ...), kind=kLoop, calls=%fused_computation.76 | loop fusion | flops 33030144 | bytes 16777216 | tf_op jit(solution)/shard_map/concatenate | solution.py:124
  601.6 13.2 %fusion.140 = f32[96,1536]{1,0:T(8,128)S(1)} fusion(f32[1536,1536]{1,0:T(8,128)} %fusion.38, s32[1536]{0:T(1024)S(1)} %copy-done.28, s32[96]{0:T(128)S(1)} %sub.151, s32[1536]{0:T(1024)S(1)} %copy-done.26, s32[96]{0:T(128)S(1)} %sub.147, f32[1536]{0:T(1024)S(1)} %select_select_fusion.5, f32[96]{0:T(128)S(1)} %compare_select_fusion.1, ...), kind=kOutput, calls=%fused_computation.241 | convolution fusion | flops 2724249600 | bytes 10053120 | tf_op jit(solution)/shard_map/dot_general | solution.py:157
  621.8 28.3 %fusion.79 = bf16[512,1536,1]{1,0,2:T(8,128)(2,1)S(1)} fusion(f32[1536,1536]{1,0:T(8,128)} %fusion.38, s32[1536]{0:T(1024)S(1)} %copy-done.28, s32[512]{0:T(512)S(1)} %dynamic_slice.42, s32[1536]{0:T(1024)S(1)} %copy-done.26, s32[512]{0:T(512)S(1)} %dynamic_slice.41, f32[1536]{0:T(1024)S(1)} %select_select_fusion.5, f32[512]{0:T(512)S(1)} %get-tuple-element.255, ...), kind=kOutput, calls=%fused_computation.131 | convolution fusion | flops 14530117632 | bytes 11042816 | tf_op jit(solution)/shard_map/dot_general | solution.py:186
  650.1 42.0 %while.21 = (s32[]{:T(128)}, f32[6,512,512]{2,1,0:T(8,128)}, s32[6]{0:T(128)S(1)}, s32[]{:T(128)}, s32[]{:T(128)}, /*index=5*/s32[6,512]{1,0:T(8,128)}, s32[512]...) while((s32[]{:T(128)}, f32[6,512,512]{2,1,0:T(8,128)}, ...), condition=%wide.region_9.12_spmd.clone, body=%wide.region_8.11_spmd.clone.sunk | while | flops 12324872 | bytes 1135325 | solution.py:184
  692.0 30.6 %all-gather.2.cloned.1.call-done = bf16[6,512,1536]{2,1,0:T(8,128)(2,1)} async-done(((bf16[6,16,1536]{2,1,0:T(8,128)(2,1)}), bf16[6,512,1536]{2,1,0:T(8,128)(2,1)}) %all-gather.2.cloned.1.call-update) | async-done | bytes 9437200 | tf_op jit(solution)/shard_map/all_gather | solution.py:189
  722.6 11.6 %convolution_subtract_fusion = f32[6,512,512]{2,1,0:T(8,128)} fusion(f32[6,512,512]{2,1,0:T(8,128)} %get-tuple-element.163, bf16[6,512,1536]{2,1,0:T(8,128)(2,1)} %all-gather.2.cloned.1.call-done, bf16[512,1536,1]{1,0,2:T(8,128)(2,1)S(1)} %fusion.79), kind=kOutput, calls=%fused_computation.132 | convolution fusion | flops 4833411072 | bytes 23592960 | tf_op jit(solution)/shard_map/sik,jk->sij/dot_general | solution.py:187
  (288 shorter events, 321.8 us)
Async XLA Ops:
  7.2 715.5 %all-gather.2.cloned.1.call-start = ((), (), s32[]{:S(2)}) async-start(), calls=%async_computation | async-start | bytes 9732096 | tf_op jit(solution)/shard_map/all_gather | solution.py:189
  25.4 18.7 %copy-start.23 = (s32[1536]{0:T(1024)}, s32[1536]{0:T(1024)S(1)}, u32[]{:S(2)}) copy-start(s32[1536]{0:T(1024)S(1)} %slice.293) | copy-start | bytes 18436
  25.6 349.9 %copy-start.2 = (f32[512,512]{1,0:T(8,128)}, f32[512,512]{1,0:T(8,128)S(1)}, u32[]{:S(2)}) copy-start(f32[512,512]{1,0:T(8,128)S(1)} %fusion.116) | copy-start | bytes 3145732
  25.7 18.5 %copy-start.29 = (s32[24576]{0:T(1024)}, s32[24576]{0:T(1024)S(1)}, u32[]{:S(2)}) copy-start(s32[24576]{0:T(1024)S(1)} %reshape_squeeze.6) | copy-start | bytes 294916
  25.7 18.5 %copy-start.25 = (s32[1536]{0:T(1024)}, s32[1536]{0:T(1024)S(1)}, u32[]{:S(2)}) copy-start(s32[1536]{0:T(1024)S(1)} %slice.295) | copy-start | bytes 18436
  25.8 18.4 %copy-start.30 = (s32[24576]{0:T(1024)}, s32[24576]{0:T(1024)S(1)}, u32[]{:S(2)}) copy-start(s32[24576]{0:T(1024)S(1)} %reshape_squeeze.7) | copy-start | bytes 294916
  25.8 18.4 %copy-start.27 = (s32[1536]{0:T(1024)}, s32[1536]{0:T(1024)S(1)}, u32[]{:S(2)}) copy-start(s32[1536]{0:T(1024)S(1)} %slice.297) | copy-start | bytes 18436
  182.3 57.6 %copy-start.4 = (f32[128,512]{1,0:T(8,128)}, f32[128,512]{1,0:T(8,128)S(1)}, u32[]{:S(2)}) copy-start(f32[128,512]{1,0:T(8,128)S(1)} %fusion.209) | copy-start | bytes 786436
  183.1 7.2 copy-start.7
  183.9 6.3 copy-start.10
  372.8 5.7 copy-start.5
  375.5 6.2 copy-start.8
  420.3 13.6 %slice-start = ((f32[384,128]{1,0:T(8,128)}), f32[128,128]{1,0:T(8,128)S(1)}, s32[]{:S(2)}) async-start(f32[384,128]{1,0:T(8,128)} %convolution_subtract_fusion.11), calls=%async_computation.1 | async-start | bytes 131072 | tf_op jit(solution)/shard_map/jit(cholesky)/cholesky | solution.py:72
  429.4 128.6 %copy-start.3 = (f32[512,512]{1,0:T(8,128)S(1)}, f32[512,512]{1,0:T(8,128)}, u32[]{:S(2)}) copy-start(f32[512,512]{1,0:T(8,128)} %copy-done.2) | copy-start | bytes 3145732
  506.3 69.4 %copy-start.20 = (s32[2,6,512]{2,0,1:T(2,128)S(1)}, s32[2,6,512]{2,0,1:T(2,128)}, u32[]{:S(2)}) copy-start(s32[2,6,512]{2,0,1:T(2,128)} %param.11) | copy-start | bytes 73732
  558.1 14.0 %copy-start.14 = (f32[512,512]{1,0:T(8,128)S(1)}, f32[512,512]{1,0:T(8,128)}, u32[]{:S(2)}) copy-start(f32[512,512]{1,0:T(8,128)} %fusion.223) | copy-start | bytes 3145732
  561.5 19.8 %copy-start.6 = (f32[128,512]{1,0:T(8,128)S(1)}, f32[128,512]{1,0:T(8,128)}, u32[]{:S(2)}) copy-start(f32[128,512]{1,0:T(8,128)} %copy-done.5) | copy-start | bytes 786436
  561.5 19.8 %copy-start.9 = (f32[128,512]{1,0:T(8,128)S(1)}, f32[128,512]{1,0:T(8,128)}, u32[]{:S(2)}) copy-start(f32[128,512]{1,0:T(8,128)} %copy-done.8) | copy-start | bytes 786436
  562.9 9.2 %copy-start.12 = (f32[128,512]{1,0:T(8,128)}, f32[128,512]{1,0:T(8,128)S(1)}, u32[]{:S(2)}) copy-start(f32[128,512]{1,0:T(8,128)S(1)} %fusion.241) | copy-start | bytes 786436
  581.2 20.4 %copy-start.24 = (s32[1536]{0:T(1024)S(1)}, s32[1536]{0:T(1024)}, u32[]{:S(2)}) copy-start(s32[1536]{0:T(1024)} %copy-done.23) | copy-start | bytes 18436
  581.2 20.4 %copy-start.26 = (s32[1536]{0:T(1024)S(1)}, s32[1536]{0:T(1024)}, u32[]{:S(2)}) copy-start(s32[1536]{0:T(1024)} %copy-done.25) | copy-start | bytes 18436
  581.2 20.4 %copy-start.28 = (s32[1536]{0:T(1024)S(1)}, s32[1536]{0:T(1024)}, u32[]{:S(2)}) copy-start(s32[1536]{0:T(1024)} %copy-done.27) | copy-start | bytes 18436
  601.5 14.9 %copy-start.15 = (f32[512,512]{1,0:T(8,128)S(1)}, f32[512,512]{1,0:T(8,128)}, u32[]{:S(2)}) copy-start(f32[512,512]{1,0:T(8,128)} %get-tuple-element.264) | copy-start | bytes 3145732
  601.6 14.9 %copy-start.16 = (f32[512,512]{1,0:T(8,128)S(1)}, f32[512,512]{1,0:T(8,128)}, u32[]{:S(2)}) copy-start(f32[512,512]{1,0:T(8,128)} %get-tuple-element.262) | copy-start | bytes 3145732
  (9 other events, 19.8 us)
Sparse Core Ops, SparseCore 0:
  619.6 102.9 all-gather.1
where the time goes:
time: 750 us; the launch traced here: 741 us
  other arithmetic  440 us (59%)
  matrix products  140 us (19%)
  local copies, waits for them, and re-layouts  76.1 us (10%)
  waiting for transfers between devices  30.6 us (4%)
  between operations  22.7 us (3%)
  blocking collectives  16 us (2%)
  loops' own time  15.8 us (2%)
    another operation x44, other arithmetic, leading_factor(): jnp.linalg.cholesky(remaining[row_begin:row_end, row_begin:row_end])  247 us
    another operation x8, other arithmetic, leading_factor(): lax.linalg.triangular_solve(diag_factor, identity, left_side=True, lower=...  127 us
    another operation x40, local copies, waits for them, and re-layouts, leading_factor(): lax.linalg.triangular_solve(diag_factor, identity, left_side=True, lower=...  30.6 us
    all_gather x1, waiting for transfers between devices, local(): lax.all_gather(panel_half, 'col', axis=1, tiled=True)  30.6 us
    dot_general x1, matrix products, local(): jnp.dot(target_cov, inverse.T, precision=highest).astype(jnp.bfloat16)  28.3 us
    another operation x18, matrix products, leading_factor(): jnp.linalg.cholesky(remaining[row_begin:row_end, row_begin:row_end])  20.6 us
    concatenate x1, other arithmetic, leading_factor(): return (jnp.concatenate(lower_rows, 0), jnp.concatenate(inverse_rows, 0))  20.2 us
    another operation x21, matrix products, leading_factor(): lax.linalg.triangular_solve(diag_factor, identity, left_side=True, lower=...  20 us
  transfers between devices with their start and end apart: 1, of which 1 were waited for; matrix products, arithmetic and copies ran while one was open for 8% of the time, Pallas kernels for 0%

commit v1 on v0

v1 whole, which is shorter than its diff:
```python
import functools, math
import jax, jax.numpy as jnp, numpy as np
from jax import lax
from jax.experimental import pallas as pl
from jax.experimental.pallas import tpu as pltpu
from jax.sharding import PartitionSpec as P
f32, bf16, i32 = jnp.float32, jnp.bfloat16, jnp.int32

TILE, LEAD, PANELS, SLOTS = 512, 1536, 3, 6
BLK, W = 128, 16
SCALE = 1.0 / (128 * 0.05)


def tables():
    bf = lambda z: np.asarray(z, np.float32).astype(bf16).astype(np.float32)
    forms = np.zeros((6, 16, 16), np.float32)
    forms[0, 0, 0] = forms[0, 1, 1] = -2.0
    forms[0, 2, 4] = forms[0, 4, 2] = 128.0
    forms[0, 3, 4] = forms[0, 5, 3] = 1.0
    sigma = (1.0, 1.3, 0.8)
    rho = {(0, 1): 0.35, (0, 2): 0.2, (1, 2): 0.3}
    shape = ((1,), (1, 1), (1, 1, 1 / 3), (1, 1, 2 / 5, 1 / 15), (1, 1, 3 / 7, 2 / 21, 1 / 105))
    for u in range(3):
        for w in range(3):
            base = (1.0 if u == w else rho[min(u, w), max(u, w)]) * sigma[u] * sigma[w]
            for d, a in enumerate(shape[u + w]):
                rest = base * a * SCALE**d
                for part in range(3):
                    top = float(bf(rest))
                    forms[1 + d, 6 + 3 * part + u, 6 + w] = top
                    rest -= top
    return forms.reshape(96, 16).astype(bf16)


def dot(a, b):
    return jnp.dot(a, b, preferred_element_type=f32)


def dot_nt(a, b):
    return lax.dot_general(a, b, (((1,), (1,)), ((), ())), preferred_element_type=f32)


def split(a):
    high = a.astype(bf16)
    return high, (a - high.astype(f32)).astype(bf16)


def features(ref):
    n = ref.shape[1]
    x, y, kind = ref[0:1, :], ref[1:2, :], ref[2:3, :]
    square = x * x + y * y
    row = lax.broadcasted_iota(i32, (16, n), 0)
    hot = jnp.where((row - 6) % 3 == kind, 1, 0)
    out = jnp.where(row >= 6, hot, 1)
    for index, value in enumerate((x, y, square >> 7, square & 127)):
        out = jnp.where(row == index, value, out)
    out = jnp.where(row == 15, 0, out)
    return out.astype(f32)


def cov(left, forms, cols):
    d2, c0, c1, c2, c3, c4 = (dot(left, forms[q, :, cols]) for q in range(6))
    t = d2 * lax.rsqrt(jnp.maximum(d2, 0.5))
    poly = (((c4 * t + c3) * t + c2) * t + c1) * t + c0
    return poly * jnp.exp2(t * (-SCALE * math.log2(math.e)))


def leaf(m_ref, n_ref):
    w = W
    row = lax.broadcasted_iota(i32, (w, BLK), 0)
    lane = lax.broadcasted_iota(i32, (w, BLK), 1)
    lane1 = lax.broadcasted_iota(i32, (1, BLK), 1)
    R = m_ref[0:w, :]
    n = BLK // w
    for s in range(n):
        K = w * s
        c = [jnp.broadcast_to(R[:, K + j:K + j + 1], (w, BLK)) for j in range(w)]
        inb = (lane >= K) & (lane < K + w)
        R = jnp.where(inb, jnp.where(lane - K == row, 1.0, 0.0), R)
        rr = jnp.zeros((w, BLK), f32)
        if s + 1 < n:
            old = m_ref[K + w:K + 2 * w, :]
            e = [jnp.broadcast_to(old[:, K + j:K + j + 1], (w, BLK)) for j in range(w)]
            nxt = jnp.where(inb, 0.0, old)
        for k in range(w):
            ck = c[k]
            r = lax.rsqrt(ck[k:k + 1, :])
            q = r * r
            Rk = R[k:k + 1, :]
            mk = jnp.where(row == k, 0.0, ck)
            n_ref[K + k:K + k + 1, :] = jnp.where(lane1 < K + w, Rk * r, 0.0)
            R = R - (mk * Rk) * q
            for j in range(k + 1, w):
                c[j] = c[j] - (mk * c[j][k:k + 1, :]) * q
            rr = jnp.where(row == k, q, rr)
        if s + 1 < n:
            T = R * rr
            acc = [None] * 4
            for j in range(w):
                v = e[j] * T[j:j + 1, :]
                acc[j % 4] = v if acc[j % 4] is None else acc[j % 4] + v
            R = nxt - ((acc[0] + acc[1]) + (acc[2] + acc[3]))
        if s + 2 < n:
            def emb(v):
                parts = [jnp.zeros((K, BLK), bf16)] if K else []
                parts += [v, jnp.zeros((BLK - K - w, BLK), bf16)]
                return jnp.concatenate(parts, 0)
            th, tl = (emb(v) for v in split(T))
            lane2 = lax.broadcasted_iota(i32, (BLK - K - 2 * w, BLK), 1)
            old = m_ref[K + 2 * w:, :]
            ah, al = split(old)
            upd = dot(ah, th) + dot(al, th) + dot(ah, tl)
            m_ref[K + 2 * w:, :] = jnp.where((lane2 >= K) & (lane2 < K + w), 0.0, old) - upd


def eye(n):
    return jnp.where(lax.broadcasted_iota(i32, (n, n), 0) == lax.broadcasted_iota(i32, (n, n), 1), 1.0, 0.0)


GC = 64


def main_kernel(where_ref, own_ref, lead_ref, target_ref, forms_ref, panel_ref, trail_ref,
                left, lead_forms, target_forms, g, vv, m_ref, n_ref, th, tl, ch, cl, pf, pj, ph, out, sems):
    row_index, col_index = where_ref[0], where_ref[1]
    forms = forms_ref[...]
    nl = LEAD
    for ref, dst, base in ((lead_ref, lead_forms, 3584), (target_ref, target_forms, 0), (own_ref, None, 512)):
        feat = features(ref)
        n = ref.shape[1]
        if dst is not None:
            all6 = dot(forms, feat.astype(bf16)).astype(bf16)
            for q in range(6):
                dst[q, :, :] = all6[16 * q:16 * q + 16, :]
        for b in range(0, n, 512):
            left[base + b:base + b + 512, :] = jnp.transpose(feat[:, b:b + 512]).astype(bf16)

    for ti in range(PANELS):
        def body(i, _, ti=ti):
            r0 = pl.multiple_of(ti * TILE + i * GC, GC)
            fl = left[pl.ds(3584 + r0, GC), :]
            for tj in range(2 * (ti + 1)):
                g[pl.ds(r0, GC), 256 * tj:256 * tj + 256] = cov(fl, lead_forms, slice(256 * tj, 256 * tj + 256))
            return 0
        lax.fori_loop(0, TILE // GC, body, 0)
    for k in range(LEAD // BLK):
        s = slice(BLK * k, BLK * k + BLK)
        g[s, s] = g[s, s] + 0.5 * eye(BLK)

    def step(k, _):
        k0 = pl.multiple_of(k * BLK, BLK)
        m_ref[...] = g[pl.ds(k0, BLK), pl.ds(k0, BLK)]
        leaf(m_ref, n_ref)
        dh, dl = split(n_ref[...])
        g[pl.ds(k0, BLK), :] = jnp.zeros((BLK, LEAD + BLK), f32)
        g[pl.ds(k0, BLK), pl.ds(k0, BLK)] = eye(BLK)
        def panel(i, _):
            r0 = pl.multiple_of(i * 512, 512)
            xh, xl = split(g[pl.ds(r0, 512), pl.ds(k0, BLK)])
            v = dot_nt(xh, dh) + dot_nt(xl, dh) + dot_nt(xh, dl)
            vh, vl = split(v)
            vv[pl.ds(r0, 512), 0:BLK] = vh
            vv[pl.ds(r0, 512), BLK:2 * BLK] = vl
            keep = lax.broadcasted_iota(i32, (512, BLK), 0) + r0 < k0 + BLK
            nh, nlo = split(jnp.where(keep, v, 0.0))
            th[pl.ds(r0, 512), pl.ds(k0, BLK)] = nh
            tl[pl.ds(r0, 512), pl.ds(k0, BLK)] = nlo
            return 0
        lax.fori_loop(0, 3, panel, 0)
        def update(j, _):
            c0 = pl.multiple_of(k0 + BLK + j * 256, BLK)
            lh = vv[pl.ds(c0, 256), 0:BLK]
            ll = vv[pl.ds(c0, 256), BLK:2 * BLK]
            l2 = jnp.concatenate([lh, lh], 1)
            def rows(i, _):
                r0 = pl.multiple_of(i * 512, 512)
                a = vv[pl.ds(r0, 512), :]
                upd = dot_nt(a, l2) + dot_nt(a[:, 0:BLK], ll)
                g[pl.ds(r0, 512), pl.ds(c0, 256)] = g[pl.ds(r0, 512), pl.ds(c0, 256)] - upd
                return 0
            lax.fori_loop(0, 3, rows, 0)
            return 0
        lax.fori_loop(0, (LEAD // BLK - k) // 2, update, 0)
        return 0
    lax.fori_loop(0, LEAD // BLK, step, 0)

    def tile(i, _):
        def gen(a, _):
            r0 = pl.multiple_of(a * GC, GC)
            fl = left[pl.ds(pl.multiple_of(i * TILE, TILE) + r0, GC), :]
            for tj in range(LEAD // 256):
                cols = slice(256 * tj, 256 * tj + 256)
                h, lo = split(cov(fl, lead_forms, cols))
                ch[pl.ds(r0, GC), cols] = h
                cl[pl.ds(r0, GC), cols] = lo
            return 0
        lax.fori_loop(0, TILE // GC, gen, 0)
        for q in range(PANELS):
            @pl.when((i == 1) & (row_index == q))
            def _():
                s = slice(TILE * q, TILE * q + TILE)
                h, lo = split(ch[:, s].astype(f32) + cl[:, s].astype(f32) + 0.5 * eye(TILE))
                ch[:, s] = h
                cl[:, s] = lo
        for u in range(LEAD // 256):
            depth = 256 * (u + 1)
            cols = slice(256 * u, depth)
            a, b = ch[:, 0:depth], cl[:, 0:depth]
            wh, wl = th[0:depth, cols], tl[0:depth, cols]
            pf[:, cols] = dot(a, wh) + dot(b, wh) + dot(a, wl)

        @pl.when(i == 0)
        def _():
            pj[...] = pf[...].astype(bf16)

        @pl.when(i > 0)
        def _():
            slot = lax.rem(i, 2)
            def store(n):
                return pltpu.make_async_copy(out.at[lax.rem(n, 2)], trail_ref.at[n - 1], sems.at[lax.rem(n, 2)])
            @pl.when(i > 2)
            def _():
                store(i - 2).wait()
            panel_ref[i - 1] = pf[pl.ds(pl.multiple_of(col_index * 16, 16), 16), :]
            ph[...] = pf[...].astype(bf16)
            def fin(a, _):
                r0 = pl.multiple_of(a * GC, GC)
                fl = left[pl.ds(pl.multiple_of(i * TILE, TILE) + r0, GC), :]
                for tj in range(TILE // 256):
                    cols = slice(256 * tj, 256 * tj + 256)
                    out[slot, pl.ds(r0, GC), cols] = cov(fl, target_forms, cols) - dot_nt(ph[pl.ds(r0, GC), :], pj[cols, :])
                return 0
            lax.fori_loop(0, TILE // GC, fin, 0)
            @pl.when((i - 1) * 8 + row_index == PANELS + col_index)
            def _():
                out[slot] = out[slot] + 0.5 * eye(TILE)
            store(i).start()
        return 0
    lax.fori_loop(0, SLOTS + 1, tile, 0)
    for n in (SLOTS - 1, SLOTS):
        pltpu.make_async_copy(out.at[n % 2], trail_ref.at[n - 1], sems.at[n % 2]).wait()


def main(where, own, lead, target, forms):
    vm = pl.BlockSpec(memory_space=pltpu.VMEM)
    scratch = [
        pltpu.VMEM((3584 + LEAD, 16), bf16),
        pltpu.VMEM((6, 16, LEAD), bf16),
        pltpu.VMEM((6, 16, TILE), bf16),
        pltpu.VMEM((LEAD, LEAD + BLK), f32),
        pltpu.VMEM((LEAD + BLK, 2 * BLK), bf16),
        pltpu.VMEM((BLK, BLK), f32),
        pltpu.VMEM((BLK, BLK), f32),
        pltpu.VMEM((LEAD, LEAD), bf16),
        pltpu.VMEM((LEAD, LEAD), bf16),
        pltpu.VMEM((TILE, LEAD), bf16),
        pltpu.VMEM((TILE, LEAD), bf16),
        pltpu.VMEM((TILE, LEAD), f32),
        pltpu.VMEM((TILE, LEAD), bf16),
        pltpu.VMEM((TILE, LEAD), bf16),
        pltpu.VMEM((2, TILE, TILE), f32),
        pltpu.SemaphoreType.DMA((2,)),
    ]
    return pl.pallas_call(
        main_kernel,
        out_shape=(jax.ShapeDtypeStruct((SLOTS, 16, LEAD), f32), jax.ShapeDtypeStruct((SLOTS, TILE, TILE), f32)),
        in_specs=[pl.BlockSpec(memory_space=pltpu.SMEM)] + [vm] * 4,
        out_specs=(vm, pl.BlockSpec(memory_space=pl.ANY)),
        scratch_shapes=scratch,
        compiler_params=pltpu.CompilerParams(vmem_limit_bytes=60 << 20),
        name="panels",
    )(where, own, lead, target, forms)


def local(grid_points, variable):
    row_index, col_index = lax.axis_index("row"), lax.axis_index("col")
    mine = jnp.concatenate([grid_points, variable[None], jnp.zeros((5,) + variable.shape, i32)], 0)
    both = jnp.moveaxis(mine[:3], 1, 0)
    everyone = lax.all_gather(both, "row", axis=1, tiled=False)
    everyone = everyone.reshape(-1, 3, TILE)
    pad = lambda z: jnp.concatenate([z, jnp.zeros((8 - z.shape[0], z.shape[1]), i32)], 0)
    lead = pad(jnp.moveaxis(everyone[:PANELS], 1, 0).reshape(3, LEAD))
    target = pad(lax.dynamic_index_in_dim(everyone, PANELS + col_index, 0, False))
    where = jnp.stack([row_index, col_index]).astype(i32)
    return main(where, mine.reshape(8, SLOTS * TILE), lead, target, jnp.asarray(tables()))


def solution(mesh):
    return jax.shard_map(
        local,
        mesh=mesh,
        in_specs=(P(None, None, "row"), P(None, "row")),
        out_specs=(P(None, ("row", "col"), None), P(None, "row", "col")),
        check_vma=False,
    )
```

time: 750 us -> 205 us (0.27); the launches traced: 741 us -> 205 us
  other arithmetic: 440 us -> 2.79 us
  Pallas kernels: 0 us -> 182 us
  matrix products: 140 us -> 0 us
  local copies, waits for them, and re-layouts: 76.1 us -> 3.09 us
  waiting for transfers between devices: 30.6 us -> 0 us
  between operations: 22.7 us -> 0.67 us
  loops' own time: 15.8 us -> 0 us
    another operation x52 -> x1, other arithmetic: 374 us -> 0.64 us  [local(): where = jnp.stack([row_index, col_index]).astype(i32)]
    pallas_call x0 -> x1, Pallas kernels: none -> 182 us  [main(): pl.pallas_call(main_kernel, out_shape=(jax.ShapeDtypeStruct((SLOTS, 16, L...]
    dot_general x14 -> x0, matrix products: 99.2 us -> none  [the longest x1 28.3 us: local(): jnp.dot(target_cov, inverse.T, precision=highest).astype(jnp.bfloat16)]
    another operation x39 -> x0, matrix products: 40.6 us -> none  [the longest x18 20.6 us: leading_factor(): jnp.linalg.cholesky(remaining[row_begin:row_end, row_begin:row_end])]
    another operation x60 -> x0, local copies, waits for them, and re-layouts: 39.7 us -> none  [the longest x40 30.6 us: leading_factor(): lax.linalg.triangular_solve(diag_factor, identity, left_side=True, lower=...]
    all_gather x1 -> x0, waiting for transfers between devices: 30.6 us -> none  [local(): lax.all_gather(panel_half, 'col', axis=1, tiled=True)]
    concatenate x2 -> x1, other arithmetic: 20.9 us -> 1.43 us  [local(): jnp.concatenate([grid_points, variable[None], jnp.zeros((5,) + variable.s...]
    add x1 -> x0, other arithmetic: 18.3 us -> none  [local(): lead_cov = lead_cov + nugget * jnp.eye(lead_size, dtype=jnp.float32)]
  transfers between devices with their start and end apart: 1 -> 0, of which waited for: 1 -> 0; matrix products, arithmetic and copies ran while one was open for 8% -> 0% of each run, Pallas kernels for 0% -> 0%
where the time goes in v1:
time: 205 us
  Pallas kernels  182 us (89%)
  blocking collectives  16 us (8%)
  local copies, waits for them, and re-layouts  3.09 us (2%)
  other arithmetic  2.79 us (1%)
    pallas_call x1, Pallas kernels, main(): pl.pallas_call(main_kernel, out_shape=(jax.ShapeDtypeStruct((SLOTS, 16, L...  182 us
    all_gather x1, blocking collectives, local(): everyone = lax.all_gather(both, 'row', axis=1, tiled=False)  16 us

profile of v1, /device:TPU:1, one launch (start us, length us, event | category | flops | bytes accessed | tf_op | source)
XLA Modules:
  0.0 204.9 jit_solution(8102999161540318558)
XLA Ops:
  0.6 0.6 pad_add_fusion.where_ref
  1.3 0.1 pad.6.clone
  1.4 0.7 copy.12
  2.1 0.7 copy.9
  2.8 0.7 add_bitcast_fusion
  3.6 1.4 add_add_fusion.own_ref
  5.0 16.0 %all-gather = s32[6,24,512]{2,0,1:T(8,128)S(1)} all-gather(s32[6,3,512]{2,0,1:T(8,128)S(1)} %add_bitcast_fusion), channel_id=2, replica_groups=mesh['row'=8,'col'=32] {'row'}, dimensions={1}, use_global_device_ids=true | all-gather | bytes 331776 | tf_op jit(solution)/shard_map/all_gather | solution.py:279
  21.0 0.2 copy.11
  21.2 0.1 reshape.15
  21.3 0.6 concatenate.22.target_ref
  21.9 0.6 concatenate.21.lead_ref
  22.5 182.4 %panels.1 = (f32[6,16,1536]{2,1,0:T(8,128)}, f32[6,512,512]{2,1,0:T(8,128)}) custom-call(s32[2]{0:T(128)} %pad_add_fusion.where_ref, s32[8,3072]{1,0:T(8,128)} %add_add_fusion.own_ref, s32[8,1536]{1,0:T(8,128)} %concatenate.21.lead_ref, s32[8,512]{1,0:T(8,128)} %concatenate.22.target_ref, bf16[96,16]{1,0:T(8,128)(2,1)} %constant.23.clone.forms_ref), custom_call_target="tpu_custom_call" | custom-call | tf_op jit(solution)/shard_map/panels/pallas_call | solution.py:264
  (3 shorter events, 0.0 us)

commit v2 on v1

v2 whole, which is shorter than its diff:
```python
import functools, math
import jax, jax.numpy as jnp, numpy as np
from jax import lax
from jax.experimental import pallas as pl
from jax.experimental.pallas import tpu as pltpu
from jax.sharding import PartitionSpec as P
f32, bf16, i32 = jnp.float32, jnp.bfloat16, jnp.int32

TILE, LEAD, PANELS, SLOTS = 512, 1536, 3, 6
BLK, W = 128, 16
SCALE = 1.0 / (128 * 0.05)


def tables():
    bf = lambda z: np.asarray(z, np.float32).astype(bf16).astype(np.float32)
    forms = np.zeros((6, 16, 16), np.float32)
    forms[0, 0, 0] = forms[0, 1, 1] = -2.0
    forms[0, 2, 4] = forms[0, 4, 2] = 128.0
    forms[0, 3, 4] = forms[0, 5, 3] = 1.0
    sigma = (1.0, 1.3, 0.8)
    rho = {(0, 1): 0.35, (0, 2): 0.2, (1, 2): 0.3}
    shape = ((1,), (1, 1), (1, 1, 1 / 3), (1, 1, 2 / 5, 1 / 15), (1, 1, 3 / 7, 2 / 21, 1 / 105))
    for u in range(3):
        for w in range(3):
            base = (1.0 if u == w else rho[min(u, w), max(u, w)]) * sigma[u] * sigma[w]
            for d, a in enumerate(shape[u + w]):
                rest = base * a * SCALE**d
                for part in range(3):
                    top = float(bf(rest))
                    forms[1 + d, 6 + 3 * part + u, 6 + w] = top
                    rest -= top
    return forms.reshape(96, 16).astype(bf16)


def dot(a, b):
    return jnp.dot(a, b, preferred_element_type=f32)


def dot_nt(a, b):
    return lax.dot_general(a, b, (((1,), (1,)), ((), ())), preferred_element_type=f32)


def split(a):
    high = a.astype(bf16)
    return high, (a - high.astype(f32)).astype(bf16)


def features(x, y, kind):
    n = x.shape[1]
    square = x * x + y * y
    row = lax.broadcasted_iota(i32, (16, n), 0)
    hot = jnp.where((row - 6) % 3 == kind, 1, 0)
    out = jnp.where(row >= 6, hot, 1)
    for index, value in enumerate((x, y, square >> 7, square & 127)):
        out = jnp.where(row == index, value, out)
    out = jnp.where(row == 15, 0, out)
    return out.astype(f32)


def cov(left, forms, cols):
    d2, c0, c1, c2, c3, c4 = (dot(left, forms[q, :, cols]) for q in range(6))
    t = d2 * lax.rsqrt(jnp.maximum(d2, 0.5))
    poly = (((c4 * t + c3) * t + c2) * t + c1) * t + c0
    return poly * jnp.exp2(t * (-SCALE * math.log2(math.e)))


def leaf(m_ref, n_ref, fill=lambda at: None):
    w = W
    row = lax.broadcasted_iota(i32, (w, BLK), 0)
    lane = lax.broadcasted_iota(i32, (w, BLK), 1)
    lane1 = lax.broadcasted_iota(i32, (1, BLK), 1)
    R = m_ref[0:w, :]
    n = BLK // w
    for s in range(n):
        K = w * s
        c = [jnp.broadcast_to(R[:, K + j:K + j + 1], (w, BLK)) for j in range(w)]
        inb = (lane >= K) & (lane < K + w)
        R = jnp.where(inb, jnp.where(lane - K == row, 1.0, 0.0), R)
        rr = jnp.zeros((w, BLK), f32)
        if s + 1 < n:
            old = m_ref[K + w:K + 2 * w, :]
            e = [jnp.broadcast_to(old[:, K + j:K + j + 1], (w, BLK)) for j in range(w)]
            nxt = jnp.where(inb, 0.0, old)
        for k in range(w):
            ck = c[k]
            r = lax.rsqrt(ck[k:k + 1, :])
            q = r * r
            Rk = R[k:k + 1, :]
            mk = jnp.where(row == k, 0.0, ck)
            n_ref[K + k:K + k + 1, :] = jnp.where(lane1 < K + w, Rk * r, 0.0)
            R = R - (mk * Rk) * q
            for j in range(k + 1, w):
                c[j] = c[j] - (mk * c[j][k:k + 1, :]) * q
            rr = jnp.where(row == k, q, rr)
            fill(K + k)
        if s + 1 < n:
            T = R * rr
            acc = [None] * 4
            for j in range(w):
                v = e[j] * T[j:j + 1, :]
                acc[j % 4] = v if acc[j % 4] is None else acc[j % 4] + v
            R = nxt - ((acc[0] + acc[1]) + (acc[2] + acc[3]))
        if s + 2 < n:
            def emb(v):
                parts = [jnp.zeros((K, BLK), bf16)] if K else []
                parts += [v, jnp.zeros((BLK - K - w, BLK), bf16)]
                return jnp.concatenate(parts, 0)
            th, tl = (emb(v) for v in split(T))
            lane2 = lax.broadcasted_iota(i32, (BLK - K - 2 * w, BLK), 1)
            old = m_ref[K + 2 * w:, :]
            ah, al = split(old)
            upd = dot(ah, th) + dot(al, th) + dot(ah, tl)
            m_ref[K + 2 * w:, :] = jnp.where((lane2 >= K) & (lane2 < K + w), 0.0, old) - upd


def eye(n):
    return jnp.where(lax.broadcasted_iota(i32, (n, n), 0) == lax.broadcasted_iota(i32, (n, n), 1), 1.0, 0.0)


RB = 4
PB = 384
U1, U2, U3 = 8, 7, 8


def main_kernel(points_ref, kinds_ref, sites_ref, forms_ref, panel_ref, trail_ref,
                left, lead_forms, target_forms, g, vv, m_ref, n_ref, dd, th, tl, ch, cl, pf, pj, ph, out, sems):
    row_index, col_index = lax.axis_index("row"), lax.axis_index("col")
    forms = forms_ref[...]
    def prepare(x, y, kind, base, dst, at):
        feat = features(x, y, kind)
        n = feat.shape[1]
        left[base:base + n, :] = jnp.transpose(feat).astype(bf16)
        if dst is not None:
            all6 = dot(forms, feat.astype(bf16)).astype(bf16)
            for q in range(6):
                dst[q, :, at:at + n] = all6[16 * q:16 * q + 16, :]
    for q in range(PANELS):
        prepare(*(sites_ref[q, d:d + 1, :] for d in range(3)), 3584 + TILE * q, lead_forms, TILE * q)
    owner = lax.rem(col_index + PANELS, sites_ref.shape[0])
    prepare(*(sites_ref[owner, d:d + 1, :] for d in range(3, 6)), 0, target_forms, 0)
    for q in range(SLOTS):
        prepare(points_ref[0, q:q + 1, :], points_ref[1, q:q + 1, :], kinds_ref[q:q + 1, :], 512 + TILE * q, None, 0)

    def lead_unit(ti, tj):
        rows, cols = slice(256 * ti, 256 * ti + 256), slice(256 * tj, 256 * tj + 256)
        block = cov(left[3584 + 256 * ti:3840 + 256 * ti, :], lead_forms, cols)
        g[rows, cols] = block + 0.5 * eye(256) if ti == tj else block

    def own_unit(n):
        r0 = pl.multiple_of(n // 6 * 256, 256)
        c0 = pl.multiple_of(lax.rem(n, 6) * 256, 256)
        h, lo = split(cov(left[pl.ds(r0, 256), :], lead_forms, pl.ds(c0, 256)))
        ch[pl.ds(r0, 256), pl.ds(c0, 256)] = h
        cl[pl.ds(r0, 256), pl.ds(c0, 256)] = lo

    def panel(p0, i):
        rows = slice(PB * i, PB * i + PB)
        xh, xl = split(g[rows, pl.ds(p0, BLK)])
        v = dot_nt(jnp.concatenate([xh, xl], 1), dd[:, 0:2 * BLK]) + dot_nt(xh, dd[:, 2 * BLK:])
        vh, vl = split(v)
        vv[rows, 0:BLK] = vh
        vv[rows, BLK:2 * BLK] = vl
        keep = lax.broadcasted_iota(i32, (PB, BLK), 0) + PB * i < p0 + BLK
        th[rows, pl.ds(p0, BLK)] = jnp.where(keep, vh, jnp.zeros_like(vh))
        tl[rows, pl.ds(p0, BLK)] = jnp.where(keep, vl, jnp.zeros_like(vl))

    def update(k0, j, blocks):
        c0 = k0 + j * 256
        cols = pl.ds(pl.multiple_of(jnp.minimum(c0, LEAD), BLK), 256)
        rows = [pl.ds(pl.multiple_of(lax.rem(c0 + n * BLK, LEAD), BLK), BLK) for n in blocks]
        lh, ll = vv[cols, 0:BLK], vv[cols, BLK:2 * BLK]
        a = jnp.concatenate([vv[r, :] for r in rows], 0)
        upd = dot_nt(a, jnp.concatenate([lh, lh], 1)) + dot_nt(a[:, 0:BLK], ll)
        for n, r in enumerate(rows):
            g[r, cols] = g[r, cols] - upd[n * BLK:n * BLK + BLK, :]

    lead_unit(0, 0)
    vv[LEAD:, :] = jnp.zeros((2 * BLK, 2 * BLK), bf16)
    m_ref[...] = g[0:BLK, 0:BLK]

    def step(slots, units, base, k, _):
        k0 = pl.multiple_of(k * BLK, BLK)
        p0 = pl.multiple_of(k * BLK - BLK, BLK)
        if slots:
            work = [functools.partial(panel, p0, i) for i in range(LEAD // PB)]
            bulk = [functools.partial(update, k0, j, range(n, min(n + RB, 12 - 2 * j))) for j in range(slots) for n in range(0, 12 - 2 * j, RB)]
            own = [lambda n=n: own_unit(k * units + base + n) for n in range(units)]
            mix = sorted([((n + 0.5) / len(bulk), f) for n, f in enumerate(bulk)] + [((n + 0.5) / len(own), f) for n, f in enumerate(own)], key=lambda z: z[0])
            work += [f for _, f in mix]
        else:
            work = [functools.partial(lead_unit, ti, tj) for ti in range(6) for tj in range(ti + 1) if ti]
        def fill(at):
            for n in range(at * len(work) // BLK, (at + 1) * len(work) // BLK):
                work[n]()
        leaf(m_ref, n_ref, fill)
        dh, dl = split(n_ref[...])
        dd[:, 0:BLK] = dh
        dd[:, BLK:2 * BLK] = dh
        dd[:, 2 * BLK:] = dl
        k1 = pl.multiple_of(jnp.minimum(k0 + BLK, LEAD - BLK), BLK)
        xh, xl = split(g[pl.ds(k1, BLK), pl.ds(k0, BLK)])
        h, lo = split(dot_nt(xh, dh) + dot_nt(xl, dh) + dot_nt(xh, dl))
        m_ref[...] = g[pl.ds(k1, BLK), pl.ds(k1, BLK)] - (dot_nt(h, h) + dot_nt(lo, h) + dot_nt(h, lo))
        g[pl.ds(k0, BLK), :] = jnp.zeros((BLK, LEAD + 2 * BLK), f32)
        g[pl.ds(k0, BLK), pl.ds(k0, BLK)] = eye(BLK)
        return 0
    step(0, 0, 0, 0, 0)
    lax.fori_loop(1, 4, functools.partial(step, 6, U1, -U1), 0)
    lax.fori_loop(4, 8, functools.partial(step, 4, U2, 3 * U1 - 4 * U2), 0)
    lax.fori_loop(8, 12, functools.partial(step, 2, U3, 3 * U1 + 4 * U2 - 8 * U3), 0)
    for i in range(LEAD // PB):
        panel(LEAD - BLK, i)

    def tile(i, _):
        t0 = pl.multiple_of(i * TILE, TILE)
        rows = pl.ds(t0, TILE)
        for q in range(PANELS):
            @pl.when((i == 1) & (row_index == q))
            def _():
                s = slice(TILE * q, TILE * q + TILE)
                h, lo = split(ch[rows, s].astype(f32) + cl[rows, s].astype(f32) + 0.5 * eye(TILE))
                ch[rows, s] = h
                cl[rows, s] = lo
        slot = lax.rem(i, 2)
        def store(n):
            return pltpu.make_async_copy(out.at[lax.rem(n, 2)], trail_ref.at[n - 1], sems.at[lax.rem(n, 2)])
        @pl.when(i > 2)
        def _():
            store(i - 2).wait()
        spot = pl.multiple_of(col_index * 16, 16)
        for u in range(LEAD // 256):
            depth = 256 * (u + 1)
            cols = slice(256 * u, depth)
            a, b = ch[rows, 0:depth], cl[rows, 0:depth]
            wh, wl = th[0:depth, cols], tl[0:depth, cols]
            pf[...] = dot(a, wh) + dot(b, wh) + dot(a, wl)
            panel_ref[jnp.maximum(i - 1, 0), :, cols] = pf[pl.ds(spot, 16), :]
            ph[:, cols] = pf[...].astype(bf16)
            if u >= 2:
                rr, cc = (u - 2) // 2 * 256, (u - 2) % 2 * 256
                fl = left[pl.ds(t0 + rr, 256), :]
                out[slot, rr:rr + 256, cc:cc + 256] = cov(fl, target_forms, slice(cc, cc + 256))

        @pl.when(i == 0)
        def _():
            pj[...] = ph[...]

        @pl.when(i > 0)
        def _():
            for tj in range(TILE // 256):
                cols = slice(256 * tj, 256 * tj + 256)
                out[slot, :, cols] = out[slot, :, cols] - dot_nt(ph[...], pj[cols, :])
            @pl.when((i - 1) * 8 + row_index == PANELS + col_index)
            def _():
                out[slot] = out[slot] + 0.5 * eye(TILE)
            store(i).start()
        return 0
    lax.fori_loop(0, SLOTS + 1, tile, 0)
    for n in (SLOTS - 1, SLOTS):
        pltpu.make_async_copy(out.at[n % 2], trail_ref.at[n - 1], sems.at[n % 2]).wait()


def exchange_kernel(send_ref, o_ref, buf, send_sem, recv_sem):
    me = lax.axis_index("row")
    count = buf.shape[0]
    other = lambda d: {"row": lax.rem(me + d, count)}
    barrier = pltpu.get_barrier_semaphore()
    for d in range(1, count):
        pl.semaphore_signal(barrier, inc=1, device_id=other(d), device_id_type=pl.DeviceIdType.MESH)
    pl.semaphore_wait(barrier, count - 1)

    def copy(d, place):
        return pltpu.make_async_remote_copy(
            src_ref=send_ref, dst_ref=buf.at[place], send_sem=send_sem.at[d - 1], recv_sem=recv_sem.at[d - 1],
            device_id=other(d), device_id_type=pl.DeviceIdType.MESH)
    for d in range(1, count):
        copy(d, me).start()
    buf[me] = send_ref[...]
    for d in range(1, count):
        copy(d, lax.rem(me + count - d, count)).wait_recv()
    for d in range(1, count):
        copy(d, me).wait_send()
    o_ref[...] = buf[...]


def exchange(send, count):
    vm = pl.BlockSpec(memory_space=pltpu.VMEM)
    shape = (count,) + send.shape
    return pl.pallas_call(
        exchange_kernel,
        out_shape=jax.ShapeDtypeStruct(shape, send.dtype),
        in_specs=[vm],
        out_specs=vm,
        scratch_shapes=[pltpu.VMEM(shape, send.dtype), pltpu.SemaphoreType.DMA((count - 1,)), pltpu.SemaphoreType.DMA((count - 1,))],
        compiler_params=pltpu.CompilerParams(collective_id=0, has_side_effects=True),
        name="exchange",
    )(send)


def main(points, kinds, sites, forms):
    vm = pl.BlockSpec(memory_space=pltpu.VMEM)
    scratch = [
        pltpu.VMEM((3584 + LEAD, 16), bf16),
        pltpu.VMEM((6, 16, LEAD), bf16),
        pltpu.VMEM((6, 16, TILE), bf16),
        pltpu.VMEM((LEAD, LEAD + 2 * BLK), f32),
        pltpu.VMEM((LEAD + 2 * BLK, 2 * BLK), bf16),
        pltpu.VMEM((BLK, BLK), f32),
        pltpu.VMEM((BLK, BLK), f32),
        pltpu.VMEM((BLK, 3 * BLK), bf16),
        pltpu.VMEM((LEAD, LEAD), bf16),
        pltpu.VMEM((LEAD, LEAD), bf16),
        pltpu.VMEM((7 * TILE, LEAD), bf16),
        pltpu.VMEM((7 * TILE, LEAD), bf16),
        pltpu.VMEM((TILE, 256), f32),
        pltpu.VMEM((TILE, LEAD), bf16),
        pltpu.VMEM((TILE, LEAD), bf16),
        pltpu.VMEM((2, TILE, TILE), f32),
        pltpu.SemaphoreType.DMA((2,)),
    ]
    return pl.pallas_call(
        main_kernel,
        out_shape=(jax.ShapeDtypeStruct((SLOTS, 16, LEAD), f32), jax.ShapeDtypeStruct((SLOTS, TILE, TILE), f32)),
        in_specs=[vm] * 4,
        out_specs=(vm, pl.BlockSpec(memory_space=pl.ANY)),
        scratch_shapes=scratch,
        compiler_params=pltpu.CompilerParams(vmem_limit_bytes=60 << 20),
        name="panels",
    )(points, kinds, sites, forms)


def local(grid_points, variable):
    count = lax.axis_size("row")
    place = (PANELS + lax.axis_index("col")) // count
    second = lax.dynamic_index_in_dim(grid_points, place, 1, False)
    kind = lax.dynamic_index_in_dim(variable, place, 0, True)
    send = jnp.concatenate([grid_points[:, 0], variable[:1], second, kind, jnp.zeros((2, TILE), i32)], 0)
    return main(grid_points, variable, exchange(send, count), jnp.asarray(tables()))


def solution(mesh):
    return jax.shard_map(
        local,
        mesh=mesh,
        in_specs=(P(None, None, "row"), P(None, "row")),
        out_specs=(P(None, ("row", "col"), None), P(None, "row", "col")),
        check_vma=False,
    )
```

time: 205 us -> 125 us (0.61)
  Pallas kernels: 182 us -> 120 us
  blocking collectives: 16 us -> 0 us
  other arithmetic: 2.79 us -> 0 us
    pallas_call x1, Pallas kernels: 182 us -> 110 us  [main(): pl.pallas_call(main_kernel, out_shape=(jax.ShapeDtypeStruct((SLOTS, 16, L...]
    all_gather x1 -> x0, blocking collectives: 16 us -> none  [local(): everyone = lax.all_gather(both, 'row', axis=1, tiled=False)]
    pallas_call x0 -> x1, Pallas kernels: none -> 10 us  [exchange(): pl.pallas_call(exchange_kernel, out_shape=jax.ShapeDtypeStruct(shape, sen...]
where the time goes in v2:
time: 125 us
  Pallas kernels  120 us (96%)
  local copies, waits for them, and re-layouts  3.55 us (3%)
    pallas_call x1, Pallas kernels, main(): pl.pallas_call(main_kernel, out_shape=(jax.ShapeDtypeStruct((SLOTS, 16, L...  110 us
    pallas_call x1, Pallas kernels, exchange(): pl.pallas_call(exchange_kernel, out_shape=jax.ShapeDtypeStruct(shape, sen...  10 us

profile of v2, /device:TPU:1, one launch (start us, length us, event | category | flops | bytes accessed | tf_op | source)
XLA Modules:
  0.0 124.9 jit_solution(15656645729627059503)
XLA Ops:
  0.6 0.8 constant_dynamic-slice_fusion
  1.4 0.8 dynamic-slice_bitcast_fusion
  2.2 0.6 concatenate.3.send_ref
  2.8 1.4 %copy.5.points_ref = s32[2,6,512]{2,1,0:T(8,128)} copy(s32[2,6,512]{2,0,1:T(2,128)} %param.3) | data formatting | bytes 49152 | tf_op args[0]
  4.2 10.0 %exchange.1.sites_ref = s32[8,8,512]{2,1,0:T(8,128)} custom-call(s32[8,512]{1,0:T(8,128)} %concatenate.3.send_ref), custom_call_target="tpu_custom_call" | custom-call | tf_op jit(solution)/shard_map/exchange/pallas_call | solution.py:289
  14.2 110.5 %panels.1 = (f32[6,16,1536]{2,1,0:T(8,128)}, f32[6,512,512]{2,1,0:T(8,128)}) custom-call(s32[2,6,512]{2,1,0:T(8,128)} %copy.5.points_ref, s32[6,512]{1,0:T(8,128)} %kinds_ref.1, s32[8,8,512]{2,1,0:T(8,128)} %exchange.1.sites_ref, bf16[96,16]{1,0:T(8,128)(2,1)} %constant.33.clone.forms_ref), custom_call_target="tpu_custom_call" | custom-call | tf_op jit(solution)/shard_map/panels/pallas_call | solution.py:321
  (1 shorter events, 0.0 us)

commit v3 on v2

--- a/solution.py
+++ b/solution.py
@@ -236,10 +236,6 @@
             pf[...] = dot(a, wh) + dot(b, wh) + dot(a, wl)
             panel_ref[jnp.maximum(i - 1, 0), :, cols] = pf[pl.ds(spot, 16), :]
             ph[:, cols] = pf[...].astype(bf16)
-            if u >= 2:
-                rr, cc = (u - 2) // 2 * 256, (u - 2) % 2 * 256
-                fl = left[pl.ds(t0 + rr, 256), :]
-                out[slot, rr:rr + 256, cc:cc + 256] = cov(fl, target_forms, slice(cc, cc + 256))
 
         @pl.when(i == 0)
         def _():
@@ -247,6 +243,9 @@
 
         @pl.when(i > 0)
         def _():
+            for rr, cc in ((0, 0), (0, 256), (256, 0), (256, 256)):
+                fl = left[pl.ds(t0 + rr, 256), :]
+                out[slot, rr:rr + 256, cc:cc + 256] = cov(fl, target_forms, slice(cc, cc + 256))
             for tj in range(TILE // 256):
                 cols = slice(256 * tj, 256 * tj + 256)
                 out[slot, :, cols] = out[slot, :, cols] - dot_nt(ph[...], pj[cols, :])

time: 125 us -> 124 us (level)
    pallas_call x1, Pallas kernels: 110 us -> 109 us  [main(): pl.pallas_call(main_kernel, out_shape=(jax.ShapeDtypeStruct((SLOTS, 16, L...]
where the time goes in v3:
time: 124 us; the launch traced here: 123 us
  Pallas kernels  119 us (96%)
  local copies, waits for them, and re-layouts  3.55 us (3%)
    pallas_call x1, Pallas kernels, main(): pl.pallas_call(main_kernel, out_shape=(jax.ShapeDtypeStruct((SLOTS, 16, L...  109 us
    pallas_call x1, Pallas kernels, exchange(): pl.pallas_call(exchange_kernel, out_shape=jax.ShapeDtypeStruct(shape, sen...  10 us

profile of v3, /device:TPU:1, one launch (start us, length us, event | category | flops | bytes accessed | tf_op | source)
XLA Modules:
  0.0 123.2 jit_solution(15250107451677329186)
XLA Ops:
  0.6 0.8 constant_dynamic-slice_fusion
  1.4 0.8 dynamic-slice_bitcast_fusion
  2.2 0.6 concatenate.3.send_ref
  2.8 1.4 %copy.5.points_ref = s32[2,6,512]{2,1,0:T(8,128)} copy(s32[2,6,512]{2,0,1:T(2,128)} %param.3) | data formatting | bytes 49152 | tf_op args[0]
  4.2 10.0 %exchange.1.sites_ref = s32[8,8,512]{2,1,0:T(8,128)} custom-call(s32[8,512]{1,0:T(8,128)} %concatenate.3.send_ref), custom_call_target="tpu_custom_call" | custom-call | tf_op jit(solution)/shard_map/exchange/pallas_call | solution.py:288
  14.2 108.8 %panels.1 = (f32[6,16,1536]{2,1,0:T(8,128)}, f32[6,512,512]{2,1,0:T(8,128)}) custom-call(s32[2,6,512]{2,1,0:T(8,128)} %copy.5.points_ref, s32[6,512]{1,0:T(8,128)} %kinds_ref.1, s32[8,8,512]{2,1,0:T(8,128)} %exchange.1.sites_ref, bf16[96,16]{1,0:T(8,128)(2,1)} %constant.33.clone.forms_ref), custom_call_target="tpu_custom_call" | custom-call | tf_op jit(solution)/shard_map/panels/pallas_call | solution.py:320
  (1 shorter events, 0.0 us)
